TPU v7x, 32 devices: a whole 2x2x4 slice. The times are simulated.
32 devices in a mesh: freq: 4 (over y, x), tile: 8 (over z, core).
Axes of the slice: x: 2, y: 2, z: 4, core: 2. Of those that a mesh axis runs over, the one named last changes fastest.
Arguments:
- x_field: bfloat16 [4, 2, 5120, 256], P('freq', None, 'tile'), may hold values from -6 to 6
- data: bfloat16 [4, 2, 5120, 256], P('freq', None, 'tile'), may hold values from -6 to 6
- u_bases: bfloat16 [4, 8, 8, 128, 2, 640], P('freq', 'tile'), may hold values from -0.21875 to 0.21875
- v_bases: bfloat16 [4, 8, 8, 128, 2, 640], P('freq', None, 'tile'), may hold values from -0.15625 to 0.15625
- ranks: int32 [4, 8, 8], P('freq'), may hold values from 49 to 96, as said below
- onset: int32 [5120, 256], P(('tile', 'freq')), may hold values from 0 to 3
Outputs:
- gradient: float32 [8, 5120, 256], P(None, ('tile', 'freq'))
Inputs may be any that keep to these rules, and one draw needn't show every extreme that they name: ranks[f,r,c] is the rank of tile (r, c) at frequency f; it is at most 96, and equal to 96 for some tile of every frequency.
All inputs are finite; a program needn't handle non-finite values.
Results may differ from a plain program's by a relative error of at most 0.0055.
Values may be sent and summed in bfloat16 or wider, within the bound.
No kernel may reach another device: no remote copies, remote signals or barrier semaphores. Data moves between devices by JAX's collectives and lax.ppermute only.
A program may use at most 64 MiB of HBM per device.

v0:
```python
import functools
import math

import jax
import jax.numpy as jnp
from jax import lax
from jax.experimental import pallas as pl
from jax.experimental.pallas import tpu as pltpu
from jax.sharding import PartitionSpec as P


RMAX = 96
LANES = 128
PARTS = 2
BF16 = jnp.bfloat16
F32 = jnp.float32
VMEM = pl.BlockSpec(memory_space=pltpu.VMEM)
SMEM = pl.BlockSpec(memory_space=pltpu.SMEM)
ANY = pl.BlockSpec(memory_space=pl.ANY)
HBM = pl.BlockSpec(memory_space=pltpu.MemorySpace.HBM)


def params():
    return pltpu.CompilerParams(vmem_limit_bytes=20 * 1024 * 1024)


def level_mask(rank):
    level = lax.broadcasted_iota(jnp.int32, (RMAX, LANES), 0)
    return (level < rank).astype(F32)


def masked(value, mask):
    copies = value.shape[1] // LANES
    return (value * jnp.concatenate([mask] * copies, axis=1)).astype(BF16)


def cost(flops):
    return pl.CostEstimate(flops=flops, bytes_accessed=10**7, transcendentals=0)


def coeff_outputs(ks, masks, factors, field, product, outs):
    stations = factors.shape[3]
    left = factors[...].reshape(len(ks) * 2 * RMAX, stations)
    half = field.shape[2] // LANES
    parts = 2 * half
    for p in range(2):
        result = jnp.dot(left, field[p], preferred_element_type=F32)
        for j in range(half):
            product[p * half + j] = result[:, j * LANES : (j + 1) * LANES]
    for i, k in enumerate(ks):
        mask = masks[i]
        base = i * 2 * RMAX
        even = [product[j, pl.ds(base, RMAX, stride=2), :] for j in range(parts)]
        odd = [product[j, pl.ds(base + 1, RMAX, stride=2), :] for j in range(parts)]
        for j in range(half):
            real = masked(even[j] + odd[half + j], mask)
            imag = masked(even[half + j] - odd[j], mask)
            outs[i][:, j * LANES : (j + 1) * LANES] = real
            outs[i][:, (half + j) * LANES : (half + j + 1) * LANES] = imag


def coeff_first_kernel(first, rest, *refs):
    rank_hbm, v_hbm, x_hbm = refs[:3]
    outs = refs[3 : 3 + len(first)]
    field, rest_factors, rest_masks = refs[3 + len(first) : 6 + len(first)]
    rank_ref, factors, product, sems, rest_sems, field_sem, rank_sem = refs[6 + len(first) :]
    me = lax.axis_index("tile")

    def load(k, target, sem):
        return pltpu.make_async_copy(v_hbm.at[me ^ k, pl.ds(0, RMAX)], target, sem)

    rank_copy = pltpu.make_async_copy(rank_hbm, rank_ref, rank_sem)
    field_copy = pltpu.make_async_copy(x_hbm, field, field_sem)
    copies = [load(k, factors.at[i], sems.at[i]) for i, k in enumerate(first)]
    rest_copies = [load(k, rest_factors.at[i], rest_sems.at[i]) for i, k in enumerate(rest)]
    field_copy.start()
    for copy in copies:
        copy.start()
    rank_copy.start()
    for copy in rest_copies:
        copy.start()
    rank_copy.wait()
    for i, k in enumerate(rest):
        rest_masks[i] = level_mask(rank_ref[me ^ k, me])
    masks = [level_mask(rank_ref[me ^ k, me]) for k in first]
    field_copy.wait()
    for copy in copies:
        copy.wait()
    coeff_outputs(first, masks, factors, field, product, outs)
    for copy in rest_copies:
        copy.wait()


def coeff_first(ranks, v, x, first, rest):
    stations, virtual = x.shape[1], x.shape[2]
    outs = [jax.ShapeDtypeStruct((RMAX, 2 * virtual), BF16) for _ in first]
    outs.append(jax.ShapeDtypeStruct(x.shape, BF16))
    outs.append(jax.ShapeDtypeStruct((len(rest), RMAX, 2, stations), BF16))
    outs.append(jax.ShapeDtypeStruct((len(rest), RMAX, LANES), F32))
    return pl.pallas_call(
        functools.partial(coeff_first_kernel, first, rest),
        out_shape=outs,
        in_specs=[HBM, HBM, HBM],
        out_specs=[VMEM for _ in outs],
        scratch_shapes=[
            pltpu.SMEM(ranks.shape, jnp.int32),
            pltpu.VMEM((len(first), RMAX, 2, stations), BF16),
            pltpu.VMEM((2 * virtual // LANES, len(first) * 2 * RMAX, LANES), F32),
            pltpu.SemaphoreType.DMA((len(first),)),
            pltpu.SemaphoreType.DMA((len(rest),)),
            pltpu.SemaphoreType.DMA,
            pltpu.SemaphoreType.DMA,
        ],
        compiler_params=params(),
        cost_estimate=cost(10**9),
        name="coeff_first",
    )(ranks, v, x)


def coeff_rest_kernel(rest, *refs):
    masks, field, factors = refs[:3]
    outs = refs[3 : 3 + len(rest)]
    coeff_outputs(rest, [masks[i] for i in range(len(rest))], factors, field, refs[-1], outs)


def coeff_rest(masks, field, factors, rest):
    width = 2 * field.shape[2]
    return pl.pallas_call(
        functools.partial(coeff_rest_kernel, rest),
        out_shape=[jax.ShapeDtypeStruct((RMAX, width), BF16) for _ in rest],
        in_specs=[VMEM, VMEM, VMEM],
        out_specs=[VMEM for _ in rest],
        scratch_shapes=[pltpu.VMEM((width // LANES, len(rest) * 2 * RMAX, LANES), F32)],
        compiler_params=params(),
        cost_estimate=cost(10**9),
        name="coeff_rest",
    )(masks, field, factors)


def prepare_kernel(want_rows, *refs):
    w_hbm, rank_ref = refs[:2]
    turned_ref = refs[3]
    if want_rows:
        rows_ref, masks = refs[4:6]
        factors, spread, paired, sems = refs[6:]
    else:
        rows_ref = masks = None
        factors, spread, paired, sems = refs[4:]
    me = lax.axis_index("tile")
    count = factors.shape[0]
    stations = factors.shape[3]
    columns = stations // LANES
    copies = [
        pltpu.make_async_copy(w_hbm.at[me ^ k, pl.ds(0, RMAX)], factors.at[k], sems.at[k])
        for k in range(count)
    ]
    for copy in copies:
        copy.start()
    if masks is not None:
        for k in range(count):
            masks[k] = level_mask(rank_ref[me, me ^ k])
    for k in range(count):
        copies[k].wait()
        flat = factors[k].reshape(2 * RMAX, stations).astype(F32)
        for j in range(columns):
            spread[j] = flat[:, j * LANES : (j + 1) * LANES]
        for p in range(2):
            for j in range(columns):
                piece = spread[j, pl.ds(p, RMAX, stride=2), :].astype(BF16)
                row = (2 * p + k % 2) * RMAX
                paired[row : row + RMAX, j * LANES : (j + 1) * LANES] = piece
                if rows_ref is not None:
                    column = p * stations + j * LANES
                    rows_ref[k * RMAX : (k + 1) * RMAX, column : column + LANES] = piece
        if k % 2:
            for i in range(4 * RMAX // LANES):
                block = paired[i * LANES : (i + 1) * LANES, :]
                turned_ref[k // 2, :, i * LANES : (i + 1) * LANES] = block.T


def prepare(w, ranks, after, want_rows):
    count, _, _, stations = w.shape
    outs = [jax.ShapeDtypeStruct((count // 2, stations, 4 * RMAX), BF16)]
    if want_rows:
        outs.append(jax.ShapeDtypeStruct((count * RMAX, 2 * stations), BF16))
        outs.append(jax.ShapeDtypeStruct((count, RMAX, LANES), F32))
    return pl.pallas_call(
        functools.partial(prepare_kernel, want_rows),
        out_shape=outs,
        in_specs=[HBM, SMEM, ANY],
        out_specs=[VMEM for _ in outs],
        scratch_shapes=[
            pltpu.VMEM((count, RMAX, 2, stations), BF16),
            pltpu.VMEM((stations // LANES, 2 * RMAX, LANES), F32),
            pltpu.VMEM((4 * RMAX, stations), BF16),
            pltpu.SemaphoreType.DMA((count,)),
        ],
        compiler_params=params(),
        cost_estimate=cost(10**9),
        name="prepare",
    )(w, ranks, after)


def apply_pairs(bases, blocks, turned_ref):
    virtual = blocks[0].shape[1] // 2
    total = None
    for i, base in enumerate(bases):
        pair = [blocks[2 * i][...], blocks[2 * i + 1][...]]
        turned = [jnp.concatenate([-b[:, virtual:], b[:, :virtual]], axis=1) for b in pair]
        stack = jnp.concatenate(pair + turned, axis=0)
        term = jnp.dot(turned_ref[base // 2], stack, preferred_element_type=F32)
        total = term if total is None else total + term
    return total


def partial_kernel(bases, *refs):
    turned_ref = refs[0]
    out_ref = refs[-1]
    out_ref[...] = apply_pairs(bases, refs[1:-1], turned_ref)


def partial_sum(turned, bases, blocks):
    stations = turned.shape[1]
    width = blocks[0].shape[1]
    return pl.pallas_call(
        functools.partial(partial_kernel, bases),
        out_shape=jax.ShapeDtypeStruct((stations, width), F32),
        in_specs=[VMEM] * (1 + len(blocks)),
        out_specs=VMEM,
        compiler_params=params(),
        cost_estimate=cost(10**9),
        name="partial_sum",
    )(turned, *blocks)


def adjoint_outputs(ks, masks, rows_ref, stacked, outs):
    low = min(ks)
    rows = rows_ref[low * RMAX : (low + len(ks)) * RMAX, :]
    product = jnp.dot(rows, stacked[...], preferred_element_type=F32)
    for i, k in enumerate(ks):
        block = product[(k - low) * RMAX : (k - low + 1) * RMAX, :]
        outs[i][...] = masked(block, masks[k])


def residual_kernel(base, ks, *refs):
    masks, rows_ref, turned_ref, data_ref, partial_ref = refs[:5]
    blocks = refs[5:7]
    outs = refs[7 : 7 + len(ks)]
    stacked = refs[7 + len(ks)]
    stations, virtual = data_ref.shape[1], data_ref.shape[2]
    predicted = partial_ref[...] + apply_pairs((base,), blocks, turned_ref)
    real = (predicted[:, :virtual] - data_ref[0].astype(F32)).astype(BF16)
    imag = (predicted[:, virtual:] - data_ref[1].astype(F32)).astype(BF16)
    stacked[:stations, :virtual] = real
    stacked[:stations, virtual:] = imag
    stacked[stations:, :virtual] = imag
    stacked[stations:, virtual:] = -real
    adjoint_outputs(ks, masks, rows_ref, stacked, outs)


def residual_blocks(masks, rows, turned, data, partial, base, blocks, ks):
    stations, virtual = data.shape[1], data.shape[2]
    outs = [jax.ShapeDtypeStruct((RMAX, 2 * virtual), BF16) for _ in ks]
    outs.append(jax.ShapeDtypeStruct((2 * stations, 2 * virtual), BF16))
    return pl.pallas_call(
        functools.partial(residual_kernel, base, ks),
        out_shape=outs,
        in_specs=[VMEM] * 7,
        out_specs=[VMEM for _ in outs],
        compiler_params=params(),
        cost_estimate=cost(10**9),
        name="residual_blocks",
    )(masks, rows, turned, data, partial, *blocks)


def adjoint_kernel(ks, *refs):
    adjoint_outputs(ks, *refs[:3], refs[3:])


def adjoint_blocks(masks, rows, stacked, ks):
    width = stacked.shape[1]
    return pl.pallas_call(
        functools.partial(adjoint_kernel, ks),
        out_shape=[jax.ShapeDtypeStruct((RMAX, width), BF16) for _ in ks],
        in_specs=[VMEM, VMEM, VMEM],
        out_specs=[VMEM for _ in ks],
        compiler_params=params(),
        cost_estimate=cost(10**9),
        name="adjoint_blocks",
    )(masks, rows, stacked)


def row_parts(share):
    small = -(-share // 40) * 16
    return [(0, share - small), (share - small, small)]


def spectrum_kernel(base, freqs, parts, *refs):
    turned_ref, partial_ref = refs[:2]
    outs = refs[4:-1]
    spectrum = refs[-1]
    mine = lax.axis_index("freq")
    spectrum[...] = partial_ref[...] + apply_pairs((base,), refs[2:4], turned_ref)
    share = spectrum.shape[0] // freqs
    for p, (start, size) in enumerate(parts):
        for k in range(freqs):
            rows = pl.ds(pl.multiple_of((mine ^ k) * share + start, 8), size)
            outs[p * freqs + k][...] = spectrum[rows, :].astype(BF16)


def spectrum_blocks(turned, partial, base, blocks, freqs):
    stations, width = partial.shape
    parts = row_parts(stations // freqs)
    outs = [jax.ShapeDtypeStruct((size, width), BF16) for _, size in parts for _ in range(freqs)]
    return pl.pallas_call(
        functools.partial(spectrum_kernel, base, freqs, parts),
        out_shape=outs,
        in_specs=[VMEM] * 4,
        out_specs=[VMEM for _ in outs],
        scratch_shapes=[pltpu.VMEM((stations, width), F32)],
        compiler_params=params(),
        cost_estimate=cost(5 * 10**8),
        name="spectrum_blocks",
    )(turned, partial, *blocks)


def traces_kernel(freqs, start, *refs):
    onset_ref = refs[0]
    blocks = refs[1 : 1 + freqs]
    out_hbm, gathered, traces, sems = refs[-4:]
    mine = lax.axis_index("freq")
    for k in range(freqs):
        gathered[mine ^ k] = blocks[k][...]
    times = 2 * freqs
    scaling = 1.0 / math.sqrt(freqs)
    size, width = blocks[0].shape
    width //= 2
    rows = pl.ds(start, size)
    copies = [
        pltpu.make_async_copy(traces.at[t], out_hbm.at[t, rows], sems.at[t])
        for t in range(times)
    ]
    onset = onset_ref[rows, :]
    for t in range(freqs):
        sums = [None, None]
        for f in range(freqs):
            turn = (f + 1) * t % times
            angle = 2.0 * math.pi * turn / times
            quarter = 4 * turn % times == 0
            for part, weight in ((0, math.cos(angle)), (1, -math.sin(angle))):
                if quarter:
                    weight = float(round(weight))
                if weight != 0.0:
                    value = gathered[f, :, part * width : (part + 1) * width]
                    term = value.astype(F32) * (weight * scaling)
                    old = sums[f % 2]
                    sums[f % 2] = term if old is None else old + term
        odd, even = sums
        traces[t] = jnp.where(t >= onset, even + odd, 0.0)
        copies[t].start()
        traces[t + freqs] = jnp.where(t + freqs >= onset, even - odd, 0.0)
        copies[t + freqs].start()
    for copy in copies:
        copy.wait()


def gated_traces(onset, blocks, start, before):
    freqs = len(blocks)
    share, virtual = onset.shape
    operands = (onset, *blocks)
    specs = [VMEM] * (1 + freqs)
    aliases = {}
    if before is not None:
        aliases = {len(operands): 0}
        operands += (before,)
        specs.append(HBM)
    return pl.pallas_call(
        functools.partial(traces_kernel, freqs, start),
        out_shape=jax.ShapeDtypeStruct((2 * freqs, share, virtual), F32),
        in_specs=specs,
        out_specs=HBM,
        scratch_shapes=[
            pltpu.VMEM((freqs, *blocks[0].shape), BF16),
            pltpu.VMEM((2 * freqs, blocks[0].shape[0], virtual), F32),
            pltpu.SemaphoreType.DMA((2 * freqs,)),
        ],
        input_output_aliases=aliases,
        compiler_params=params(),
        cost_estimate=cost(5 * 10**8),
        name="gated_traces",
    )(*operands)


def send(block, axis, k):
    count = lax.axis_size(axis)
    return lax.ppermute(block, axis, [(i, i ^ k) for i in range(count)])


def exchange(ks, blocks):
    return {k: send(b, "tile", k) if k else b for k, b in zip(ks, blocks)}


def pick(arrived, bases):
    return [arrived[base + b] for base in bases for b in range(2)]


def pair_bases(count):
    return list(range(count - 2, -1, -2))


def peer_order(count):
    far = [base + b for base in pair_bases(count) if base >= count // 2 for b in range(2)]
    near = [base + b for base in pair_bases(count) if 0 < base < count // 2 for b in range(2)]
    return tuple(far[:2]), tuple(far[2:3] + near + far[3:] + [1, 0])


def hbm(array):
    return pltpu.with_memory_space_constraint(array, pltpu.MemorySpace.HBM)


def body(x_field, data, u_bases, v_bases, ranks, onset):
    count = lax.axis_size("tile")
    freqs = lax.axis_size("freq")
    table = ranks[0]
    u = hbm(u_bases[0, 0])
    v = hbm(v_bases[0, :, 0])
    x = hbm(x_field[0])
    late = count // 2
    early = tuple(base for base in pair_bases(count) if base != late)
    first, rest = peer_order(count)
    *blocks, field, rest_factors, rest_masks = coeff_first(hbm(table), v, x, first, rest)
    arrived = exchange(first, blocks)
    blocks = coeff_rest(rest_masks, field, rest_factors, rest)
    arrived |= exchange(rest, blocks)
    u_turned, u_rows, masks = prepare(u, table, blocks[0], True)
    partial = partial_sum(u_turned, early, pick(arrived, early))
    *blocks, stacked = residual_blocks(
        masks, u_rows, u_turned, data[0], partial, late, pick(arrived, (late,)), first
    )
    returned = exchange(first, blocks)
    blocks = adjoint_blocks(masks, u_rows, stacked, rest)
    returned |= exchange(rest, blocks)
    (v_turned,) = prepare(v, table, stacked, False)
    late = first[0]
    early = tuple(base for base in pair_bases(count) if base != late)
    partial = partial_sum(v_turned, early, pick(returned, early))
    blocks = spectrum_blocks(v_turned, partial, late, pick(returned, (late,)), freqs)
    spectra = []
    for p in range(PARTS):
        part = blocks[p * freqs : (p + 1) * freqs]
        spectra.append([send(b, "freq", k) if k else b for k, b in enumerate(part)])
    result = None
    for p, (start, _) in enumerate(row_parts(onset.shape[0])):
        result = gated_traces(onset, spectra[p], start, result)
    return result


def solution(mesh):
    in_specs = (
        P("freq", None, "tile", None),
        P("freq", None, "tile", None),
        P("freq", "tile", None, None, None, None),
        P("freq", None, "tile", None, None, None),
        P("freq", None, None),
        P(("tile", "freq"), None),
    )
    out_specs = P(None, ("tile", "freq"), None)

    return jax.shard_map(body, mesh=mesh, in_specs=in_specs, out_specs=out_specs, check_vma=False)
```

profile of v0, /device:TPU:0, one launch (start us, length us, event | category | flops | bytes accessed | tf_op | source)
XLA Modules:
  0.0 60.8 jit_solution(14106630079502355671)
XLA Ops:
  0.0 2.4 %coeff_first.1 = (bf16[96,512]{1,0:T(8,128)(2,1)S(1)}, bf16[96,512]{1,0:T(8,128)(2,1)S(1)}, bf16[2,640,256]{2,1,0:T(8,128)(2,1)S(1)}, bf16[6,96,2,640]{3,2,1,0:T(2,128)(2,1)S(1)}, f32[6,96,128]{2,1,0:T(8,128)S(1)}) custom-call(s32[8,8]{1,0:T(8,128)} %bitcast.6, bf16[8,128,2,640]{3,2,1,0:T(2,128)(2,1)} %bitcast.9, bf16[2,640,256]{2,1,0:T(8,128)(2,1)} %bitcast.12), custom_call_target="tpu_custom_call" | custom-call | flops 1000000000 | bytes 10000000 | tf_op jit(solution)/shard_map/coeff_first/pallas_call | solution.py:100
  2.4 1.3 %coeff_rest.1 = (bf16[96,512]{1,0:T(8,128)(2,1)S(1)}, bf16[96,512]{1,0:T(8,128)(2,1)S(1)}, bf16[96,512]{1,0:T(8,128)(2,1)S(1)}, bf16[96,512]{1,0:T(8,128)(2,1)S(...) custom-call(f32[6,96,128]{2,1,0:T(8,128)S(1)} %get-tuple-element.36.refs_0_, ...), custom_call_target="tpu_custom_call" | custom-call | flops 1000000000 | bytes 10000000 | tf_op jit(solution)/shard_map/coeff_rest/pallas_call | solution.py:128
  3.6 3.1 %collective-permute-start.2 = (bf16[96,512]{1,0:T(8,128)(2,1)S(1)}, bf16[96,512]{1,0:T(8,128)(2,1)S(1)}, u32[]{:S(2)}, u32[]{:S(2)}) collective-permute-start(bf16[96,512]{1,0:T(8,128)(2,1)S(1)} %get-tuple-element.45), channel_id=1, source_target_pairs={{0,2},{1,3},{2,0},{3,1},{4,6},{5,7},{6,4},{7,5},{8,10},{9,11},{10,... | collective-permute-start | bytes 294920 | tf_op jit(solution)/shard_map/ppermute | solution.py:396
  7.0 4.0 %collective-permute-start = (bf16[96,512]{1,0:T(8,128)(2,1)S(1)}, bf16[96,512]{1,0:T(8,128)(2,1)S(1)}, u32[]{:S(2)}, u32[]{:S(2)}) collective-permute-start(bf16[96,512]{1,0:T(8,128)(2,1)S(1)} %get-tuple-element.43), channel_id=1, source_target_pairs={{0,6},{1,7},{2,4},{3,5},{4,2},{5,3},{6,0},{7,1},{8,14},{9,15},{10,... | collective-permute-start | bytes 294920 | tf_op jit(solution)/shard_map/ppermute | solution.py:396
  10.9 0.7 %collective-permute-start.6 = (bf16[96,512]{1,0:T(8,128)(2,1)S(1)}, bf16[96,512]{1,0:T(8,128)(2,1)S(1)}, u32[]{:S(2)}, u32[]{:S(2)}) collective-permute-start(bf16[96,512]{1,0:T(8,128)(2,1)S(1)} %get-tuple-element.49), channel_id=1, source_target_pairs={{0,5},{1,4},{2,7},{3,6},{4,1},{5,0},{6,3},{7,2},{8,13},{9,12},{10,... | collective-permute-start | bytes 294920 | tf_op jit(solution)/shard_map/ppermute | solution.py:396
  11.7 2.8 %collective-permute-start.5 = (bf16[96,512]{1,0:T(8,128)(2,1)S(1)}, bf16[96,512]{1,0:T(8,128)(2,1)S(1)}, u32[]{:S(2)}, u32[]{:S(2)}) collective-permute-start(bf16[96,512]{1,0:T(8,128)(2,1)S(1)} %get-tuple-element.39.refs_2_), channel_id=1, source_target_pairs={{0,4},{1,5},{2,6},{3,7},{4,0},{5,1},{6,2},{7,3},{8,12},{9,13},{10,... | collective-permute-start | bytes 294920 | tf_op jit(solution)/shard_map/ppermute | solution.py:396
  14.4 4.1 %prepare.2 = (bf16[4,640,384]{2,1,0:T(8,128)(2,1)S(1)}, bf16[768,1280]{1,0:T(8,128)(2,1)S(1)}, f32[8,96,128]{2,1,0:T(8,128)S(1)}) custom-call(bf16[8,128,2,640]{3,2,1,0:T(2,128)(2,1)} %bitcast.11, s32[8,8]{1,0:T(8,128)S(1)} %bitcast.7, bf16[96,512]{1,0:T(8,128)(2,1)S(1)} %get-tuple-element.39.refs_2_), custom_call_target="tpu_custom_call" | custom-call | flops 1000000000 | bytes 10000000 | tf_op jit(solution)/shard_map/prepare/pallas_call | solution.py:187
  18.6 1.2 %partial_sum.2.refs_4_ = f32[640,512]{1,0:T(8,128)S(1)} custom-call(bf16[4,640,384]{2,1,0:T(8,128)(2,1)S(1)} %get-tuple-element.42.refs_0_.refs_2_, bf16[96,512]{1,0:T(8,128)(2,1)S(1)} %collective-permute-done.refs_1_, bf16[96,512]{1,0:T(8,128)(2,1)S(1)} %collective-permute-done.1.refs_2_, bf16[96,512]{1,0:T(8,128)(2,1)S(1)} %collective-permute-done.2.refs_3_, ...), custom_call_target="tpu_custom_call" | custom-call | flops 1000000000 | bytes 10000000 | tf_op jit(solution)/shard_map/partial_sum/pallas_call | solution.py:225
  19.7 5.8 %collective-permute-done.6.refs_6_ = bf16[96,512]{1,0:T(8,128)(2,1)S(1)} collective-permute-done((bf16[96,512]{1,0:T(8,128)(2,1)S(1)}, bf16[96,512]{1,0:T(8,128)(2,1)S(1)}, u32[]{:S(2)}, u32[]{:S(2)}) %collective-permute-start.6) | collective-permute-done | bytes 98336 | tf_op jit(solution)/shard_map/ppermute | solution.py:396
  25.5 2.2 %collective-permute-done.5.refs_5_ = bf16[96,512]{1,0:T(8,128)(2,1)S(1)} collective-permute-done((bf16[96,512]{1,0:T(8,128)(2,1)S(1)}, bf16[96,512]{1,0:T(8,128)(2,1)S(1)}, u32[]{:S(2)}, u32[]{:S(2)}) %collective-permute-start.5) | collective-permute-done | bytes 98336 | tf_op jit(solution)/shard_map/ppermute | solution.py:396
  27.8 0.9 %residual_blocks.1 = (bf16[96,512]{1,0:T(8,128)(2,1)S(1)}, bf16[96,512]{1,0:T(8,128)(2,1)S(1)}, bf16[1280,512]{1,0:T(8,128)(2,1)S(1)}) custom-call(f32[8,96,128]{2,1,0:T(8,128)S(1)} %get-tuple-element.40.refs_0_, bf16[768,1280]{1,0:T(8,128)(2,1)S(1)} %get-tuple-element.41.refs_1_, bf16[4,640,384]{2,1,0:T(8,128)(2,1)S(1)} %get-tuple-element.42.refs_0_.refs_2_, ...), custom_call_target="tpu_custom_call" | custom-call | flops 1000000000 | bytes 10000000 | tf_op jit(solution)/shard_map/residual_blocks/pallas_call | solution.py:265
  28.6 0.9 %adjoint_blocks.1 = (bf16[96,512]{1,0:T(8,128)(2,1)S(1)}, bf16[96,512]{1,0:T(8,128)(2,1)S(1)}, bf16[96,512]{1,0:T(8,128)(2,1)S(1)}, bf16[96,512]{1,0:T(8,128)(2,...) custom-call(f32[8,96,128]{2,1,0:T(8,128)S(1)} %get-tuple-element.40.refs_0_, ...), custom_call_target="tpu_custom_call" | custom-call | flops 1000000000 | bytes 10000000 | tf_op jit(solution)/shard_map/adjoint_blocks/pallas_call | solution.py:282
  29.7 2.2 %collective-permute-start.8 = (bf16[96,512]{1,0:T(8,128)(2,1)S(1)}, bf16[96,512]{1,0:T(8,128)(2,1)S(1)}, u32[]{:S(2)}, u32[]{:S(2)}) collective-permute-start(bf16[96,512]{1,0:T(8,128)(2,1)S(1)} %get-tuple-element.52), channel_id=1, source_target_pairs={{0,5},{1,4},{2,7},{3,6},{4,1},{5,0},{6,3},{7,2},{8,13},{9,12},{10,... | collective-permute-start | bytes 294920 | tf_op jit(solution)/shard_map/ppermute | solution.py:396
  31.9 0.8 %collective-permute-start.9 = (bf16[96,512]{1,0:T(8,128)(2,1)S(1)}, bf16[96,512]{1,0:T(8,128)(2,1)S(1)}, u32[]{:S(2)}, u32[]{:S(2)}) collective-permute-start(bf16[96,512]{1,0:T(8,128)(2,1)S(1)} %get-tuple-element.53), channel_id=1, source_target_pairs={{0,2},{1,3},{2,0},{3,1},{4,6},{5,7},{6,4},{7,5},{8,10},{9,11},{10,... | collective-permute-start | bytes 294920 | tf_op jit(solution)/shard_map/ppermute | solution.py:396
  32.7 1.3 %collective-permute-start.10 = (bf16[96,512]{1,0:T(8,128)(2,1)S(1)}, bf16[96,512]{1,0:T(8,128)(2,1)S(1)}, u32[]{:S(2)}, u32[]{:S(2)}) collective-permute-start(bf16[96,512]{1,0:T(8,128)(2,1)S(1)} %get-tuple-element.54), channel_id=1, source_target_pairs={{0,3},{1,2},{2,1},{3,0},{4,7},{5,6},{6,5},{7,4},{8,11},{9,10},{10,... | collective-permute-start | bytes 294920 | tf_op jit(solution)/shard_map/ppermute | solution.py:396
  34.0 5.1 %collective-permute-done.7.refs_1_ = bf16[96,512]{1,0:T(8,128)(2,1)S(1)} collective-permute-done((bf16[96,512]{1,0:T(8,128)(2,1)S(1)}, bf16[96,512]{1,0:T(8,128)(2,1)S(1)}, u32[]{:S(2)}, u32[]{:S(2)}) %collective-permute-start.7) | collective-permute-done | bytes 98336 | tf_op jit(solution)/shard_map/ppermute | solution.py:396
  39.1 1.8 %collective-permute-start.12 = (bf16[96,512]{1,0:T(8,128)(2,1)S(1)}, bf16[96,512]{1,0:T(8,128)(2,1)S(1)}, u32[]{:S(2)}, u32[]{:S(2)}) collective-permute-start(bf16[96,512]{1,0:T(8,128)(2,1)S(1)} %get-tuple-element.57), channel_id=1, source_target_pairs={{0,6},{1,7},{2,4},{3,5},{4,2},{5,3},{6,0},{7,1},{8,14},{9,15},{10,... | collective-permute-start | bytes 294920 | tf_op jit(solution)/shard_map/ppermute | solution.py:396
  40.9 1.5 %collective-permute-start.13 = (bf16[96,512]{1,0:T(8,128)(2,1)S(1)}, bf16[96,512]{1,0:T(8,128)(2,1)S(1)}, u32[]{:S(2)}, u32[]{:S(2)}) collective-permute-start(bf16[96,512]{1,0:T(8,128)(2,1)S(1)} %get-tuple-element.58), channel_id=1, source_target_pairs={{0,7},{1,6},{2,5},{3,4},{4,3},{5,2},{6,1},{7,0},{8,15},{9,14},{10,... | collective-permute-start | bytes 294920 | tf_op jit(solution)/shard_map/ppermute | solution.py:396
  42.4 3.9 %prepare.3.refs_0_ = bf16[4,640,384]{2,1,0:T(8,128)(2,1)S(1)} custom-call(bf16[8,128,2,640]{3,2,1,0:T(2,128)(2,1)} %bitcast.10, s32[8,8]{1,0:T(8,128)S(1)} %bitcast.8, bf16[1280,512]{1,0:T(8,128)(2,1)S(1)} %get-tuple-element.50.refs_2_), custom_call_target="tpu_custom_call" | custom-call | flops 1000000000 | bytes 10000000 | tf_op jit(solution)/shard_map/prepare/pallas_call | solution.py:187
  46.3 1.2 %partial_sum.3.refs_1_ = f32[640,512]{1,0:T(8,128)S(1)} custom-call(bf16[4,640,384]{2,1,0:T(8,128)(2,1)S(1)} %prepare.3.refs_0_, bf16[96,512]{1,0:T(8,128)(2,1)S(1)} %collective-permute-done.7.refs_1_, bf16[96,512]{1,0:T(8,128)(2,1)S(1)} %collective-permute-done.8.refs_2_, bf16[96,512]{1,0:T(8,128)(2,1)S(1)} %collective-permute-done.9.refs_3_, ...), custom_call_target="tpu_custom_call" | custom-call | flops 1000000000 | bytes 10000000 | tf_op jit(solution)/shard_map/partial_sum/pallas_call | solution.py:225
  47.5 0.6 %spectrum_blocks.1 = (bf16[96,512]{1,0:T(8,128)(2,1)S(1)}, bf16[96,512]{1,0:T(8,128)(2,1)S(1)}, bf16[96,512]{1,0:T(8,128)(2,1)S(1)}, bf16[96,512]{1,0:T(8,128)(2...) custom-call(bf16[4,640,384]{2,1,0:T(8,128)(2,1)S(1)} %prepare.3.refs, ...), custom_call_target="tpu_custom_call" | custom-call | flops 500000000 | bytes 10000000 | tf_op jit(solution)/shard_map/spectrum_blocks/pallas_call | solution.py:315
  48.2 1.6 %collective-permute-start.17 = (bf16[96,512]{1,0:T(8,128)(2,1)S(1)}, bf16[96,512]{1,0:T(8,128)(2,1)S(1)}, u32[]{:S(2)}, u32[]{:S(2)}) collective-permute-start(bf16[96,512]{1,0:T(8,128)(2,1)S(1)} %get-tuple-element.64), channel_id=1, source_target_pairs={{0,8},{8,0},{16,24},{24,16},{1,9},{9,1},{17,25},{25,17},{2,10},{10... | collective-permute-start | bytes 294920 | tf_op jit(solution)/shard_map/ppermute | solution.py:396
  49.7 1.5 %collective-permute-start.18 = (bf16[96,512]{1,0:T(8,128)(2,1)S(1)}, bf16[96,512]{1,0:T(8,128)(2,1)S(1)}, u32[]{:S(2)}, u32[]{:S(2)}) collective-permute-start(bf16[96,512]{1,0:T(8,128)(2,1)S(1)} %get-tuple-element.65), channel_id=1, source_target_pairs={{0,16},{8,24},{16,0},{24,8},{1,17},{9,25},{17,1},{25,9},{2,18},{10... | collective-permute-start | bytes 294920 | tf_op jit(solution)/shard_map/ppermute | solution.py:396
  51.2 0.5 collective-permute-start.19
  51.7 1.5 %collective-permute-start.14 = (bf16[64,512]{1,0:T(8,128)(2,1)S(1)}, bf16[64,512]{1,0:T(8,128)(2,1)S(1)}, u32[]{:S(2)}, u32[]{:S(2)}) collective-permute-start(bf16[64,512]{1,0:T(8,128)(2,1)S(1)} %get-tuple-element.60), channel_id=1, source_target_pairs={{0,8},{8,0},{16,24},{24,16},{1,9},{9,1},{17,25},{25,17},{2,10},{10... | collective-permute-start | bytes 196616 | tf_op jit(solution)/shard_map/ppermute | solution.py:396
  53.2 1.5 %collective-permute-start.15 = (bf16[64,512]{1,0:T(8,128)(2,1)S(1)}, bf16[64,512]{1,0:T(8,128)(2,1)S(1)}, u32[]{:S(2)}, u32[]{:S(2)}) collective-permute-start(bf16[64,512]{1,0:T(8,128)(2,1)S(1)} %get-tuple-element.61), channel_id=1, source_target_pairs={{0,16},{8,24},{16,0},{24,8},{1,17},{9,25},{17,1},{25,9},{2,18},{10... | collective-permute-start | bytes 196616 | tf_op jit(solution)/shard_map/ppermute | solution.py:396
  54.7 1.6 %collective-permute-start.16 = (bf16[64,512]{1,0:T(8,128)(2,1)S(1)}, bf16[64,512]{1,0:T(8,128)(2,1)S(1)}, u32[]{:S(2)}, u32[]{:S(2)}) collective-permute-start(bf16[64,512]{1,0:T(8,128)(2,1)S(1)} %get-tuple-element.62), channel_id=1, source_target_pairs={{0,24},{8,16},{16,8},{24,0},{1,25},{9,17},{17,9},{25,1},{2,26},{10... | collective-permute-start | bytes 196616 | tf_op jit(solution)/shard_map/ppermute | solution.py:396
  56.3 0.2 collective-permute-done.18.refs_3_
  56.6 1.2 %collective-permute-done.19.refs_4_ = bf16[96,512]{1,0:T(8,128)(2,1)S(1)} collective-permute-done((bf16[96,512]{1,0:T(8,128)(2,1)S(1)}, bf16[96,512]{1,0:T(8,128)(2,1)S(1)}, u32[]{:S(2)}, u32[]{:S(2)}) %collective-permute-start.19) | collective-permute-done | bytes 98336 | tf_op jit(solution)/shard_map/ppermute | solution.py:396
  57.8 1.0 %gated_traces.2.refs_5_ = f32[8,160,256]{2,1,0:T(8,128)} custom-call(s32[160,256]{1,0:T(8,128)S(1)} %copy-done, bf16[96,512]{1,0:T(8,128)(2,1)S(1)} %get-tuple-element.63.refs_1_, bf16[96,512]{1,0:T(8,128)(2,1)S(1)} %collective-permute-done.17.refs_2_, bf16[96,512]{1,0:T(8,128)(2,1)S(1)} %collective-permute-done.18.refs_3_, ...), custom_call_target="tpu_custom_call" | custom-call | flops 500000000 | bytes 10000000 | tf_op jit(solution)/shard_map/gated_traces/pallas_call | solution.py:377
  59.1 0.8 %collective-permute-done.16.refs_4_ = bf16[64,512]{1,0:T(8,128)(2,1)S(1)} collective-permute-done((bf16[64,512]{1,0:T(8,128)(2,1)S(1)}, bf16[64,512]{1,0:T(8,128)(2,1)S(1)}, u32[]{:S(2)}, u32[]{:S(2)}) %collective-permute-start.16) | collective-permute-done | bytes 65568 | tf_op jit(solution)/shard_map/ppermute | solution.py:396
  59.9 0.9 %gated_traces.3 = f32[8,160,256]{2,1,0:T(8,128)} custom-call(s32[160,256]{1,0:T(8,128)S(1)} %copy-done, bf16[64,512]{1,0:T(8,128)(2,1)S(1)} %get-tuple-element.59.refs_1_, bf16[64,512]{1,0:T(8,128)(2,1)S(1)} %collective-permute-done.14.refs_2_, bf16[64,512]{1,0:T(8,128)(2,1)S(1)} %collective-permute-done.15.refs_3_, ...), custom_call_target="tpu_custom_call", output_to_operand_aliasing={{}: (5, {})} | custom-call | flops 500000000 | bytes 10000000 | tf_op jit(solution)/shard_map/gated_traces/pallas_call | solution.py:377
  (25 shorter events, 0.5 us)
Async XLA Ops:
  2.4 12.1 %copy-start.2 = (s32[1,8,8]{2,1,0:T(8,128)S(1)}, s32[1,8,8]{2,1,0:T(8,128)}, u32[]{:S(2)}) copy-start(s32[1,8,8]{2,1,0:T(8,128)} %param.10) | copy-start | bytes 772
  3.6 7.3 %collective-permute-start.2 = (bf16[96,512]{1,0:T(8,128)(2,1)S(1)}, bf16[96,512]{1,0:T(8,128)(2,1)S(1)}, u32[]{:S(2)}, u32[]{:S(2)}) collective-permute-start(bf16[96,512]{1,0:T(8,128)(2,1)S(1)} %get-tuple-element.45), channel_id=1, source_target_pairs={{0,2},{1,3},{2,0},{3,1},{4,6},{5,7},{6,4},{7,5},{8,10},{9,11},{10,... | collective-permute-start | bytes 294920 | tf_op jit(solution)/shard_map/ppermute | solution.py:396
  6.8 4.9 %collective-permute-start.3 = (bf16[96,512]{1,0:T(8,128)(2,1)S(1)}, bf16[96,512]{1,0:T(8,128)(2,1)S(1)}, u32[]{:S(2)}, u32[]{:S(2)}) collective-permute-start(bf16[96,512]{1,0:T(8,128)(2,1)S(1)} %get-tuple-element.46), channel_id=1, source_target_pairs={{0,3},{1,2},{2,1},{3,0},{4,7},{5,6},{6,5},{7,4},{8,11},{9,10},{10,... | collective-permute-start | bytes 294920 | tf_op jit(solution)/shard_map/ppermute | solution.py:396
  6.8 11.8 %collective-permute-start.4 = (bf16[96,512]{1,0:T(8,128)(2,1)S(1)}, bf16[96,512]{1,0:T(8,128)(2,1)S(1)}, u32[]{:S(2)}, u32[]{:S(2)}) collective-permute-start(bf16[96,512]{1,0:T(8,128)(2,1)S(1)} %get-tuple-element.48), channel_id=1, source_target_pairs={{0,1},{1,0},{2,3},{3,2},{4,5},{5,4},{6,7},{7,6},{8,9},{9,8},{10,11... | collective-permute-start | bytes 294920 | tf_op jit(solution)/shard_map/ppermute | solution.py:396
  7.0 11.6 %collective-permute-start = (bf16[96,512]{1,0:T(8,128)(2,1)S(1)}, bf16[96,512]{1,0:T(8,128)(2,1)S(1)}, u32[]{:S(2)}, u32[]{:S(2)}) collective-permute-start(bf16[96,512]{1,0:T(8,128)(2,1)S(1)} %get-tuple-element.43), channel_id=1, source_target_pairs={{0,6},{1,7},{2,4},{3,5},{4,2},{5,3},{6,0},{7,1},{8,14},{9,15},{10,... | collective-permute-start | bytes 294920 | tf_op jit(solution)/shard_map/ppermute | solution.py:396
  10.9 7.6 %collective-permute-start.1 = (bf16[96,512]{1,0:T(8,128)(2,1)S(1)}, bf16[96,512]{1,0:T(8,128)(2,1)S(1)}, u32[]{:S(2)}, u32[]{:S(2)}) collective-permute-start(bf16[96,512]{1,0:T(8,128)(2,1)S(1)} %get-tuple-element.44), channel_id=1, source_target_pairs={{0,7},{1,6},{2,5},{3,4},{4,3},{5,2},{6,1},{7,0},{8,15},{9,14},{10,... | collective-permute-start | bytes 294920 | tf_op jit(solution)/shard_map/ppermute | solution.py:396
  10.9 14.6 %collective-permute-start.6 = (bf16[96,512]{1,0:T(8,128)(2,1)S(1)}, bf16[96,512]{1,0:T(8,128)(2,1)S(1)}, u32[]{:S(2)}, u32[]{:S(2)}) collective-permute-start(bf16[96,512]{1,0:T(8,128)(2,1)S(1)} %get-tuple-element.49), channel_id=1, source_target_pairs={{0,5},{1,4},{2,7},{3,6},{4,1},{5,0},{6,3},{7,2},{8,13},{9,12},{10,... | collective-permute-start | bytes 294920 | tf_op jit(solution)/shard_map/ppermute | solution.py:396
  11.7 16.1 %collective-permute-start.5 = (bf16[96,512]{1,0:T(8,128)(2,1)S(1)}, bf16[96,512]{1,0:T(8,128)(2,1)S(1)}, u32[]{:S(2)}, u32[]{:S(2)}) collective-permute-start(bf16[96,512]{1,0:T(8,128)(2,1)S(1)} %get-tuple-element.39.refs_2_), channel_id=1, source_target_pairs={{0,4},{1,5},{2,6},{3,7},{4,0},{5,1},{6,2},{7,3},{8,12},{9,13},{10,... | collective-permute-start | bytes 294920 | tf_op jit(solution)/shard_map/ppermute | solution.py:396
  18.5 9.2 %copy-start.1 = (bf16[1,2,640,256]{3,2,1,0:T(8,128)(2,1)S(1)}, bf16[1,2,640,256]{3,2,1,0:T(8,128)(2,1)}, u32[]{:S(2)}) copy-start(bf16[1,2,640,256]{3,2,1,0:T(8,128)(2,1)} %param.7) | copy-start | bytes 1966084
  29.6 9.6 %collective-permute-start.7 = (bf16[96,512]{1,0:T(8,128)(2,1)S(1)}, bf16[96,512]{1,0:T(8,128)(2,1)S(1)}, u32[]{:S(2)}, u32[]{:S(2)}) collective-permute-start(bf16[96,512]{1,0:T(8,128)(2,1)S(1)} %get-tuple-element.51), channel_id=1, source_target_pairs={{0,4},{1,5},{2,6},{3,7},{4,0},{5,1},{6,2},{7,3},{8,12},{9,13},{10,... | collective-permute-start | bytes 294920 | tf_op jit(solution)/shard_map/ppermute | solution.py:396
  29.7 11.2 %collective-permute-start.8 = (bf16[96,512]{1,0:T(8,128)(2,1)S(1)}, bf16[96,512]{1,0:T(8,128)(2,1)S(1)}, u32[]{:S(2)}, u32[]{:S(2)}) collective-permute-start(bf16[96,512]{1,0:T(8,128)(2,1)S(1)} %get-tuple-element.52), channel_id=1, source_target_pairs={{0,5},{1,4},{2,7},{3,6},{4,1},{5,0},{6,3},{7,2},{8,13},{9,12},{10,... | collective-permute-start | bytes 294920 | tf_op jit(solution)/shard_map/ppermute | solution.py:396
  31.9 14.4 %collective-permute-start.9 = (bf16[96,512]{1,0:T(8,128)(2,1)S(1)}, bf16[96,512]{1,0:T(8,128)(2,1)S(1)}, u32[]{:S(2)}, u32[]{:S(2)}) collective-permute-start(bf16[96,512]{1,0:T(8,128)(2,1)S(1)} %get-tuple-element.53), channel_id=1, source_target_pairs={{0,2},{1,3},{2,0},{3,1},{4,6},{5,7},{6,4},{7,5},{8,10},{9,11},{10,... | collective-permute-start | bytes 294920 | tf_op jit(solution)/shard_map/ppermute | solution.py:396
  32.7 13.6 %collective-permute-start.10 = (bf16[96,512]{1,0:T(8,128)(2,1)S(1)}, bf16[96,512]{1,0:T(8,128)(2,1)S(1)}, u32[]{:S(2)}, u32[]{:S(2)}) collective-permute-start(bf16[96,512]{1,0:T(8,128)(2,1)S(1)} %get-tuple-element.54), channel_id=1, source_target_pairs={{0,3},{1,2},{2,1},{3,0},{4,7},{5,6},{6,5},{7,4},{8,11},{9,10},{10,... | collective-permute-start | bytes 294920 | tf_op jit(solution)/shard_map/ppermute | solution.py:396
  34.0 12.3 %collective-permute-start.11 = (bf16[96,512]{1,0:T(8,128)(2,1)S(1)}, bf16[96,512]{1,0:T(8,128)(2,1)S(1)}, u32[]{:S(2)}, u32[]{:S(2)}) collective-permute-start(bf16[96,512]{1,0:T(8,128)(2,1)S(1)} %get-tuple-element.56), channel_id=1, source_target_pairs={{0,1},{1,0},{2,3},{3,2},{4,5},{5,4},{6,7},{7,6},{8,9},{9,8},{10,11... | collective-permute-start | bytes 294920 | tf_op jit(solution)/shard_map/ppermute | solution.py:396
  39.1 8.4 %collective-permute-start.12 = (bf16[96,512]{1,0:T(8,128)(2,1)S(1)}, bf16[96,512]{1,0:T(8,128)(2,1)S(1)}, u32[]{:S(2)}, u32[]{:S(2)}) collective-permute-start(bf16[96,512]{1,0:T(8,128)(2,1)S(1)} %get-tuple-element.57), channel_id=1, source_target_pairs={{0,6},{1,7},{2,4},{3,5},{4,2},{5,3},{6,0},{7,1},{8,14},{9,15},{10,... | collective-permute-start | bytes 294920 | tf_op jit(solution)/shard_map/ppermute | solution.py:396
  40.9 6.6 %collective-permute-start.13 = (bf16[96,512]{1,0:T(8,128)(2,1)S(1)}, bf16[96,512]{1,0:T(8,128)(2,1)S(1)}, u32[]{:S(2)}, u32[]{:S(2)}) collective-permute-start(bf16[96,512]{1,0:T(8,128)(2,1)S(1)} %get-tuple-element.58), channel_id=1, source_target_pairs={{0,7},{1,6},{2,5},{3,4},{4,3},{5,2},{6,1},{7,0},{8,15},{9,14},{10,... | collective-permute-start | bytes 294920 | tf_op jit(solution)/shard_map/ppermute | solution.py:396
  47.5 10.3 %copy-start = (s32[160,256]{1,0:T(8,128)S(1)}, s32[160,256]{1,0:T(8,128)}, u32[]{:S(2)}) copy-start(s32[160,256]{1,0:T(8,128)} %refs_0_.3) | copy-start | bytes 491524
  48.2 6.6 %collective-permute-start.17 = (bf16[96,512]{1,0:T(8,128)(2,1)S(1)}, bf16[96,512]{1,0:T(8,128)(2,1)S(1)}, u32[]{:S(2)}, u32[]{:S(2)}) collective-permute-start(bf16[96,512]{1,0:T(8,128)(2,1)S(1)} %get-tuple-element.64), channel_id=1, source_target_pairs={{0,8},{8,0},{16,24},{24,16},{1,9},{9,1},{17,25},{25,17},{2,10},{10... | collective-permute-start | bytes 294920 | tf_op jit(solution)/shard_map/ppermute | solution.py:396
  49.7 6.8 %collective-permute-start.18 = (bf16[96,512]{1,0:T(8,128)(2,1)S(1)}, bf16[96,512]{1,0:T(8,128)(2,1)S(1)}, u32[]{:S(2)}, u32[]{:S(2)}) collective-permute-start(bf16[96,512]{1,0:T(8,128)(2,1)S(1)} %get-tuple-element.65), channel_id=1, source_target_pairs={{0,16},{8,24},{16,0},{24,8},{1,17},{9,25},{17,1},{25,9},{2,18},{10... | collective-permute-start | bytes 294920 | tf_op jit(solution)/shard_map/ppermute | solution.py:396
  51.2 6.6 %collective-permute-start.19 = (bf16[96,512]{1,0:T(8,128)(2,1)S(1)}, bf16[96,512]{1,0:T(8,128)(2,1)S(1)}, u32[]{:S(2)}, u32[]{:S(2)}) collective-permute-start(bf16[96,512]{1,0:T(8,128)(2,1)S(1)} %get-tuple-element.66), channel_id=1, source_target_pairs={{0,24},{8,16},{16,8},{24,0},{1,25},{9,17},{17,9},{25,1},{2,26},{10... | collective-permute-start | bytes 294920 | tf_op jit(solution)/shard_map/ppermute | solution.py:396
  51.7 7.1 %collective-permute-start.14 = (bf16[64,512]{1,0:T(8,128)(2,1)S(1)}, bf16[64,512]{1,0:T(8,128)(2,1)S(1)}, u32[]{:S(2)}, u32[]{:S(2)}) collective-permute-start(bf16[64,512]{1,0:T(8,128)(2,1)S(1)} %get-tuple-element.60), channel_id=1, source_target_pairs={{0,8},{8,0},{16,24},{24,16},{1,9},{9,1},{17,25},{25,17},{2,10},{10... | collective-permute-start | bytes 196616 | tf_op jit(solution)/shard_map/ppermute | solution.py:396
  53.2 5.9 %collective-permute-start.15 = (bf16[64,512]{1,0:T(8,128)(2,1)S(1)}, bf16[64,512]{1,0:T(8,128)(2,1)S(1)}, u32[]{:S(2)}, u32[]{:S(2)}) collective-permute-start(bf16[64,512]{1,0:T(8,128)(2,1)S(1)} %get-tuple-element.61), channel_id=1, source_target_pairs={{0,16},{8,24},{16,0},{24,8},{1,17},{9,25},{17,1},{25,9},{2,18},{10... | collective-permute-start | bytes 196616 | tf_op jit(solution)/shard_map/ppermute | solution.py:396
  54.7 5.2 %collective-permute-start.16 = (bf16[64,512]{1,0:T(8,128)(2,1)S(1)}, bf16[64,512]{1,0:T(8,128)(2,1)S(1)}, u32[]{:S(2)}, u32[]{:S(2)}) collective-permute-start(bf16[64,512]{1,0:T(8,128)(2,1)S(1)} %get-tuple-element.62), channel_id=1, source_target_pairs={{0,24},{8,16},{16,8},{24,0},{1,25},{9,17},{17,9},{25,1},{2,26},{10... | collective-permute-start | bytes 196616 | tf_op jit(solution)/shard_map/ppermute | solution.py:396
where the time goes:
time: 61 us; the launch traced here: 60.8 us
  starting transfers between devices  26.7 us (44%)
  Pallas kernels  18.3 us (30%)
  waiting for transfers between devices  15.7 us (26%)
    ppermute x20, starting transfers between devices, send(): return lax.ppermute(block, axis, [(i, i ^ k) for i in range(count)])  26.7 us
    ppermute x20, waiting for transfers between devices, send(): return lax.ppermute(block, axis, [(i, i ^ k) for i in range(count)])  15.7 us
    pallas_call x2, Pallas kernels, prepare(): pl.pallas_call(functools.partial(prepare_kernel, want_rows), out_shape=ou...  7.97 us
    pallas_call x2, Pallas kernels, partial_sum(): pl.pallas_call(functools.partial(partial_kernel, bases), out_shape=jax.Sh...  2.35 us
    pallas_call x1, Pallas kernels, coeff_first(): pl.pallas_call(functools.partial(coeff_first_kernel, first, rest), out_sh...  2.35 us
    pallas_call x2, Pallas kernels, gated_traces(): pl.pallas_call(functools.partial(traces_kernel, freqs, start), out_shape=...  1.94 us
    pallas_call x1, Pallas kernels, coeff_rest(): pl.pallas_call(functools.partial(coeff_rest_kernel, rest), out_shape=[jax...  1.26 us
  transfers between devices with their start and end apart: 20, of which 7 were waited for; matrix products, arithmetic and copies ran while one was open for 0% of the time, Pallas kernels for 19%

commit v1 on v0

--- a/solution.py
+++ b/solution.py
@@ -22,6 +22,19 @@
 
 def params():
     return pltpu.CompilerParams(vmem_limit_bytes=20 * 1024 * 1024)
+
+
+def swapped(k, freqs):
+    bits = freqs.bit_length() - 1
+    if bits % 2:
+        return k
+    half = bits // 2
+    return (k % (1 << half) << half) | (k >> half)
+
+
+def freq_peer(k, freqs):
+    turn = jnp.where(lax.axis_index("tile") % 2 == 1, k, swapped(k, freqs))
+    return lax.axis_index("freq") ^ turn
 
 
 def level_mask(rank):
@@ -299,12 +312,11 @@
     turned_ref, partial_ref = refs[:2]
     outs = refs[4:-1]
     spectrum = refs[-1]
-    mine = lax.axis_index("freq")
     spectrum[...] = partial_ref[...] + apply_pairs((base,), refs[2:4], turned_ref)
     share = spectrum.shape[0] // freqs
     for p, (start, size) in enumerate(parts):
         for k in range(freqs):
-            rows = pl.ds(pl.multiple_of((mine ^ k) * share + start, 8), size)
+            rows = pl.ds(pl.multiple_of(freq_peer(k, freqs) * share + start, 8), size)
             outs[p * freqs + k][...] = spectrum[rows, :].astype(BF16)
 
 
@@ -328,9 +340,8 @@
     onset_ref = refs[0]
     blocks = refs[1 : 1 + freqs]
     out_hbm, gathered, traces, sems = refs[-4:]
-    mine = lax.axis_index("freq")
     for k in range(freqs):
-        gathered[mine ^ k] = blocks[k][...]
+        gathered[freq_peer(k, freqs)] = blocks[k][...]
     times = 2 * freqs
     scaling = 1.0 / math.sqrt(freqs)
     size, width = blocks[0].shape
@@ -396,6 +407,17 @@
     return lax.ppermute(block, axis, [(i, i ^ k) for i in range(count)])
 
 
+def send_freq(block, k):
+    count = lax.axis_size("tile")
+    freqs = lax.axis_size("freq")
+    pairs = [
+        (f * count + tile, (f ^ (k if tile % 2 else swapped(k, freqs))) * count + tile)
+        for f in range(freqs)
+        for tile in range(count)
+    ]
+    return lax.ppermute(block, ("freq", "tile"), pairs)
+
+
 def exchange(ks, blocks):
     return {k: send(b, "tile", k) if k else b for k, b in zip(ks, blocks)}
 
@@ -448,7 +470,7 @@
     spectra = []
     for p in range(PARTS):
         part = blocks[p * freqs : (p + 1) * freqs]
-        spectra.append([send(b, "freq", k) if k else b for k, b in enumerate(part)])
+        spectra.append([send_freq(b, k) if k else b for k, b in enumerate(part)])
     result = None
     for p, (start, _) in enumerate(row_parts(onset.shape[0])):
         result = gated_traces(onset, spectra[p], start, result)

time: 61 us -> 61 us (level)
  waiting for transfers between devices: 15.7 us -> 14.6 us
  starting transfers between devices: 26.7 us -> 27.7 us
    ppermute x0 -> x6, starting transfers between devices: none -> 9.23 us  [send_freq(): return lax.ppermute(block, ('freq', 'tile'), pairs)]
    ppermute x20 -> x14, starting transfers between devices: 26.7 us -> 18.5 us  [send(): return lax.ppermute(block, axis, [(i, i ^ k) for i in range(count)])]
    ppermute x20 -> x14, waiting for transfers between devices: 15.7 us -> 13.2 us  [send(): return lax.ppermute(block, axis, [(i, i ^ k) for i in range(count)])]
    ppermute x0 -> x6, waiting for transfers between devices: none -> 1.46 us  [send_freq(): return lax.ppermute(block, ('freq', 'tile'), pairs)]
  transfers between devices with their start and end apart: 20 -> 20, of which waited for: 7 -> 6; matrix products, arithmetic and copies ran while one was open for 0% -> 0% of each run, Pallas kernels for 19% -> 19%
where the time goes in v1:
time: 61 us; the launch traced here: 60.8 us
  starting transfers between devices  27.7 us (45%)
  Pallas kernels  18.3 us (30%)
  waiting for transfers between devices  14.6 us (24%)
    ppermute x14, starting transfers between devices, send(): return lax.ppermute(block, axis, [(i, i ^ k) for i in range(count)])  18.5 us
    ppermute x14, waiting for transfers between devices, send(): return lax.ppermute(block, axis, [(i, i ^ k) for i in range(count)])  13.2 us
    ppermute x6, starting transfers between devices, send_freq(): return lax.ppermute(block, ('freq', 'tile'), pairs)  9.23 us
    pallas_call x2, Pallas kernels, prepare(): pl.pallas_call(functools.partial(prepare_kernel, want_rows), out_shape=ou...  7.97 us
    pallas_call x2, Pallas kernels, partial_sum(): pl.pallas_call(functools.partial(partial_kernel, bases), out_shape=jax.Sh...  2.35 us
    pallas_call x1, Pallas kernels, coeff_first(): pl.pallas_call(functools.partial(coeff_first_kernel, first, rest), out_sh...  2.35 us
    pallas_call x2, Pallas kernels, gated_traces(): pl.pallas_call(functools.partial(traces_kernel, freqs, start), out_shape=...  1.94 us
    ppermute x6, waiting for transfers between devices, send_freq(): return lax.ppermute(block, ('freq', 'tile'), pairs)  1.46 us
  transfers between devices with their start and end apart: 20, of which 6 were waited for; matrix products, arithmetic and copies ran while one was open for 0% of the time, Pallas kernels for 19%

profile of v1, /device:TPU:0, one launch (start us, length us, event | category | flops | bytes accessed | tf_op | source)
XLA Modules:
  0.0 60.8 jit_solution(15989881980263884090)
XLA Ops:
  0.0 2.4 %coeff_first.1 = (bf16[96,512]{1,0:T(8,128)(2,1)S(1)}, bf16[96,512]{1,0:T(8,128)(2,1)S(1)}, bf16[2,640,256]{2,1,0:T(8,128)(2,1)S(1)}, bf16[6,96,2,640]{3,2,1,0:T(2,128)(2,1)S(1)}, f32[6,96,128]{2,1,0:T(8,128)S(1)}) custom-call(s32[8,8]{1,0:T(8,128)} %bitcast.6, bf16[8,128,2,640]{3,2,1,0:T(2,128)(2,1)} %bitcast.9, bf16[2,640,256]{2,1,0:T(8,128)(2,1)} %bitcast.12), custom_call_target="tpu_custom_call" | custom-call | flops 1000000000 | bytes 10000000 | tf_op jit(solution)/shard_map/coeff_first/pallas_call | solution.py:113
  2.4 1.3 %coeff_rest.1 = (bf16[96,512]{1,0:T(8,128)(2,1)S(1)}, bf16[96,512]{1,0:T(8,128)(2,1)S(1)}, bf16[96,512]{1,0:T(8,128)(2,1)S(1)}, bf16[96,512]{1,0:T(8,128)(2,1)S(...) custom-call(f32[6,96,128]{2,1,0:T(8,128)S(1)} %get-tuple-element.36.refs_0_, ...), custom_call_target="tpu_custom_call" | custom-call | flops 1000000000 | bytes 10000000 | tf_op jit(solution)/shard_map/coeff_rest/pallas_call | solution.py:141
  3.6 3.1 %collective-permute-start.2 = (bf16[96,512]{1,0:T(8,128)(2,1)S(1)}, bf16[96,512]{1,0:T(8,128)(2,1)S(1)}, u32[]{:S(2)}, u32[]{:S(2)}) collective-permute-start(bf16[96,512]{1,0:T(8,128)(2,1)S(1)} %get-tuple-element.45), channel_id=1, source_target_pairs={{0,2},{1,3},{2,0},{3,1},{4,6},{5,7},{6,4},{7,5},{8,10},{9,11},{10,... | collective-permute-start | bytes 294920 | tf_op jit(solution)/shard_map/ppermute | solution.py:407
  7.0 4.0 %collective-permute-start = (bf16[96,512]{1,0:T(8,128)(2,1)S(1)}, bf16[96,512]{1,0:T(8,128)(2,1)S(1)}, u32[]{:S(2)}, u32[]{:S(2)}) collective-permute-start(bf16[96,512]{1,0:T(8,128)(2,1)S(1)} %get-tuple-element.43), channel_id=1, source_target_pairs={{0,6},{1,7},{2,4},{3,5},{4,2},{5,3},{6,0},{7,1},{8,14},{9,15},{10,... | collective-permute-start | bytes 294920 | tf_op jit(solution)/shard_map/ppermute | solution.py:407
  10.9 0.7 %collective-permute-start.6 = (bf16[96,512]{1,0:T(8,128)(2,1)S(1)}, bf16[96,512]{1,0:T(8,128)(2,1)S(1)}, u32[]{:S(2)}, u32[]{:S(2)}) collective-permute-start(bf16[96,512]{1,0:T(8,128)(2,1)S(1)} %get-tuple-element.49), channel_id=1, source_target_pairs={{0,5},{1,4},{2,7},{3,6},{4,1},{5,0},{6,3},{7,2},{8,13},{9,12},{10,... | collective-permute-start | bytes 294920 | tf_op jit(solution)/shard_map/ppermute | solution.py:407
  11.7 2.8 %collective-permute-start.5 = (bf16[96,512]{1,0:T(8,128)(2,1)S(1)}, bf16[96,512]{1,0:T(8,128)(2,1)S(1)}, u32[]{:S(2)}, u32[]{:S(2)}) collective-permute-start(bf16[96,512]{1,0:T(8,128)(2,1)S(1)} %get-tuple-element.39.refs_2_), channel_id=1, source_target_pairs={{0,4},{1,5},{2,6},{3,7},{4,0},{5,1},{6,2},{7,3},{8,12},{9,13},{10,... | collective-permute-start | bytes 294920 | tf_op jit(solution)/shard_map/ppermute | solution.py:407
  14.4 4.1 %prepare.2 = (bf16[4,640,384]{2,1,0:T(8,128)(2,1)S(1)}, bf16[768,1280]{1,0:T(8,128)(2,1)S(1)}, f32[8,96,128]{2,1,0:T(8,128)S(1)}) custom-call(bf16[8,128,2,640]{3,2,1,0:T(2,128)(2,1)} %bitcast.11, s32[8,8]{1,0:T(8,128)S(1)} %bitcast.7, bf16[96,512]{1,0:T(8,128)(2,1)S(1)} %get-tuple-element.39.refs_2_), custom_call_target="tpu_custom_call" | custom-call | flops 1000000000 | bytes 10000000 | tf_op jit(solution)/shard_map/prepare/pallas_call | solution.py:200
  18.6 1.2 %partial_sum.2.refs_4_ = f32[640,512]{1,0:T(8,128)S(1)} custom-call(bf16[4,640,384]{2,1,0:T(8,128)(2,1)S(1)} %get-tuple-element.42.refs_0_.refs_2_, bf16[96,512]{1,0:T(8,128)(2,1)S(1)} %collective-permute-done.refs_1_, bf16[96,512]{1,0:T(8,128)(2,1)S(1)} %collective-permute-done.1.refs_2_, bf16[96,512]{1,0:T(8,128)(2,1)S(1)} %collective-permute-done.2.refs_3_, ...), custom_call_target="tpu_custom_call" | custom-call | flops 1000000000 | bytes 10000000 | tf_op jit(solution)/shard_map/partial_sum/pallas_call | solution.py:238
  19.7 5.8 %collective-permute-done.6.refs_6_ = bf16[96,512]{1,0:T(8,128)(2,1)S(1)} collective-permute-done((bf16[96,512]{1,0:T(8,128)(2,1)S(1)}, bf16[96,512]{1,0:T(8,128)(2,1)S(1)}, u32[]{:S(2)}, u32[]{:S(2)}) %collective-permute-start.6) | collective-permute-done | bytes 98336 | tf_op jit(solution)/shard_map/ppermute | solution.py:407
  25.5 2.2 %collective-permute-done.5.refs_5_ = bf16[96,512]{1,0:T(8,128)(2,1)S(1)} collective-permute-done((bf16[96,512]{1,0:T(8,128)(2,1)S(1)}, bf16[96,512]{1,0:T(8,128)(2,1)S(1)}, u32[]{:S(2)}, u32[]{:S(2)}) %collective-permute-start.5) | collective-permute-done | bytes 98336 | tf_op jit(solution)/shard_map/ppermute | solution.py:407
  27.8 0.9 %residual_blocks.1 = (bf16[96,512]{1,0:T(8,128)(2,1)S(1)}, bf16[96,512]{1,0:T(8,128)(2,1)S(1)}, bf16[1280,512]{1,0:T(8,128)(2,1)S(1)}) custom-call(f32[8,96,128]{2,1,0:T(8,128)S(1)} %get-tuple-element.40.refs_0_, bf16[768,1280]{1,0:T(8,128)(2,1)S(1)} %get-tuple-element.41.refs_1_, bf16[4,640,384]{2,1,0:T(8,128)(2,1)S(1)} %get-tuple-element.42.refs_0_.refs_2_, ...), custom_call_target="tpu_custom_call" | custom-call | flops 1000000000 | bytes 10000000 | tf_op jit(solution)/shard_map/residual_blocks/pallas_call | solution.py:278
  28.6 0.9 %adjoint_blocks.1 = (bf16[96,512]{1,0:T(8,128)(2,1)S(1)}, bf16[96,512]{1,0:T(8,128)(2,1)S(1)}, bf16[96,512]{1,0:T(8,128)(2,1)S(1)}, bf16[96,512]{1,0:T(8,128)(2,...) custom-call(f32[8,96,128]{2,1,0:T(8,128)S(1)} %get-tuple-element.40.refs_0_, ...), custom_call_target="tpu_custom_call" | custom-call | flops 1000000000 | bytes 10000000 | tf_op jit(solution)/shard_map/adjoint_blocks/pallas_call | solution.py:295
  29.7 2.2 %collective-permute-start.8 = (bf16[96,512]{1,0:T(8,128)(2,1)S(1)}, bf16[96,512]{1,0:T(8,128)(2,1)S(1)}, u32[]{:S(2)}, u32[]{:S(2)}) collective-permute-start(bf16[96,512]{1,0:T(8,128)(2,1)S(1)} %get-tuple-element.52), channel_id=1, source_target_pairs={{0,5},{1,4},{2,7},{3,6},{4,1},{5,0},{6,3},{7,2},{8,13},{9,12},{10,... | collective-permute-start | bytes 294920 | tf_op jit(solution)/shard_map/ppermute | solution.py:407
  31.9 0.8 %collective-permute-start.9 = (bf16[96,512]{1,0:T(8,128)(2,1)S(1)}, bf16[96,512]{1,0:T(8,128)(2,1)S(1)}, u32[]{:S(2)}, u32[]{:S(2)}) collective-permute-start(bf16[96,512]{1,0:T(8,128)(2,1)S(1)} %get-tuple-element.53), channel_id=1, source_target_pairs={{0,2},{1,3},{2,0},{3,1},{4,6},{5,7},{6,4},{7,5},{8,10},{9,11},{10,... | collective-permute-start | bytes 294920 | tf_op jit(solution)/shard_map/ppermute | solution.py:407
  32.7 1.3 %collective-permute-start.10 = (bf16[96,512]{1,0:T(8,128)(2,1)S(1)}, bf16[96,512]{1,0:T(8,128)(2,1)S(1)}, u32[]{:S(2)}, u32[]{:S(2)}) collective-permute-start(bf16[96,512]{1,0:T(8,128)(2,1)S(1)} %get-tuple-element.54), channel_id=1, source_target_pairs={{0,3},{1,2},{2,1},{3,0},{4,7},{5,6},{6,5},{7,4},{8,11},{9,10},{10,... | collective-permute-start | bytes 294920 | tf_op jit(solution)/shard_map/ppermute | solution.py:407
  34.0 5.1 %collective-permute-done.7.refs_1_ = bf16[96,512]{1,0:T(8,128)(2,1)S(1)} collective-permute-done((bf16[96,512]{1,0:T(8,128)(2,1)S(1)}, bf16[96,512]{1,0:T(8,128)(2,1)S(1)}, u32[]{:S(2)}, u32[]{:S(2)}) %collective-permute-start.7) | collective-permute-done | bytes 98336 | tf_op jit(solution)/shard_map/ppermute | solution.py:407
  39.1 1.8 %collective-permute-start.12 = (bf16[96,512]{1,0:T(8,128)(2,1)S(1)}, bf16[96,512]{1,0:T(8,128)(2,1)S(1)}, u32[]{:S(2)}, u32[]{:S(2)}) collective-permute-start(bf16[96,512]{1,0:T(8,128)(2,1)S(1)} %get-tuple-element.57), channel_id=1, source_target_pairs={{0,6},{1,7},{2,4},{3,5},{4,2},{5,3},{6,0},{7,1},{8,14},{9,15},{10,... | collective-permute-start | bytes 294920 | tf_op jit(solution)/shard_map/ppermute | solution.py:407
  40.9 1.5 %collective-permute-start.13 = (bf16[96,512]{1,0:T(8,128)(2,1)S(1)}, bf16[96,512]{1,0:T(8,128)(2,1)S(1)}, u32[]{:S(2)}, u32[]{:S(2)}) collective-permute-start(bf16[96,512]{1,0:T(8,128)(2,1)S(1)} %get-tuple-element.58), channel_id=1, source_target_pairs={{0,7},{1,6},{2,5},{3,4},{4,3},{5,2},{6,1},{7,0},{8,15},{9,14},{10,... | collective-permute-start | bytes 294920 | tf_op jit(solution)/shard_map/ppermute | solution.py:407
  42.4 3.9 %prepare.3.refs_0_ = bf16[4,640,384]{2,1,0:T(8,128)(2,1)S(1)} custom-call(bf16[8,128,2,640]{3,2,1,0:T(2,128)(2,1)} %bitcast.10, s32[8,8]{1,0:T(8,128)S(1)} %bitcast.8, bf16[1280,512]{1,0:T(8,128)(2,1)S(1)} %get-tuple-element.50.refs_2_), custom_call_target="tpu_custom_call" | custom-call | flops 1000000000 | bytes 10000000 | tf_op jit(solution)/shard_map/prepare/pallas_call | solution.py:200
  46.3 1.2 %partial_sum.3.refs_1_ = f32[640,512]{1,0:T(8,128)S(1)} custom-call(bf16[4,640,384]{2,1,0:T(8,128)(2,1)S(1)} %prepare.3.refs_0_, bf16[96,512]{1,0:T(8,128)(2,1)S(1)} %collective-permute-done.7.refs_1_, bf16[96,512]{1,0:T(8,128)(2,1)S(1)} %collective-permute-done.8.refs_2_, bf16[96,512]{1,0:T(8,128)(2,1)S(1)} %collective-permute-done.9.refs_3_, ...), custom_call_target="tpu_custom_call" | custom-call | flops 1000000000 | bytes 10000000 | tf_op jit(solution)/shard_map/partial_sum/pallas_call | solution.py:238
  47.5 0.6 %spectrum_blocks.1 = (bf16[96,512]{1,0:T(8,128)(2,1)S(1)}, bf16[96,512]{1,0:T(8,128)(2,1)S(1)}, bf16[96,512]{1,0:T(8,128)(2,1)S(1)}, bf16[96,512]{1,0:T(8,128)(2...) custom-call(bf16[4,640,384]{2,1,0:T(8,128)(2,1)S(1)} %prepare.3.refs, ...), custom_call_target="tpu_custom_call" | custom-call | flops 500000000 | bytes 10000000 | tf_op jit(solution)/shard_map/spectrum_blocks/pallas_call | solution.py:327
  48.2 1.6 %collective-permute-start.17 = (bf16[96,512]{1,0:T(8,128)(2,1)S(1)}, bf16[96,512]{1,0:T(8,128)(2,1)S(1)}, u32[]{:S(2)}, u32[]{:S(2)}) collective-permute-start(bf16[96,512]{1,0:T(8,128)(2,1)S(1)} %get-tuple-element.64), channel_id=1, source_target_pairs={{0,16},{1,9},{2,18},{3,11},{4,20},{5,13},{6,22},{7,15},{8,24},{9,1... | collective-permute-start | bytes 294920 | tf_op jit(solution)/shard_map/ppermute | solution.py:418
  49.8 1.5 %collective-permute-start.18 = (bf16[96,512]{1,0:T(8,128)(2,1)S(1)}, bf16[96,512]{1,0:T(8,128)(2,1)S(1)}, u32[]{:S(2)}, u32[]{:S(2)}) collective-permute-start(bf16[96,512]{1,0:T(8,128)(2,1)S(1)} %get-tuple-element.65), channel_id=1, source_target_pairs={{0,8},{1,17},{2,10},{3,19},{4,12},{5,21},{6,14},{7,23},{8,0},{9,25... | collective-permute-start | bytes 294920 | tf_op jit(solution)/shard_map/ppermute | solution.py:418
  51.2 0.5 collective-permute-start.19
  51.7 1.5 %collective-permute-start.14 = (bf16[64,512]{1,0:T(8,128)(2,1)S(1)}, bf16[64,512]{1,0:T(8,128)(2,1)S(1)}, u32[]{:S(2)}, u32[]{:S(2)}) collective-permute-start(bf16[64,512]{1,0:T(8,128)(2,1)S(1)} %get-tuple-element.60), channel_id=1, source_target_pairs={{0,16},{1,9},{2,18},{3,11},{4,20},{5,13},{6,22},{7,15},{8,24},{9,1... | collective-permute-start | bytes 196616 | tf_op jit(solution)/shard_map/ppermute | solution.py:418
  53.2 1.5 %collective-permute-start.15 = (bf16[64,512]{1,0:T(8,128)(2,1)S(1)}, bf16[64,512]{1,0:T(8,128)(2,1)S(1)}, u32[]{:S(2)}, u32[]{:S(2)}) collective-permute-start(bf16[64,512]{1,0:T(8,128)(2,1)S(1)} %get-tuple-element.61), channel_id=1, source_target_pairs={{0,8},{1,17},{2,10},{3,19},{4,12},{5,21},{6,14},{7,23},{8,0},{9,25... | collective-permute-start | bytes 196616 | tf_op jit(solution)/shard_map/ppermute | solution.py:418
  54.7 2.7 %collective-permute-start.16 = (bf16[64,512]{1,0:T(8,128)(2,1)S(1)}, bf16[64,512]{1,0:T(8,128)(2,1)S(1)}, u32[]{:S(2)}, u32[]{:S(2)}) collective-permute-start(bf16[64,512]{1,0:T(8,128)(2,1)S(1)} %get-tuple-element.62), channel_id=1, source_target_pairs={{0,24},{1,25},{2,26},{3,27},{4,28},{5,29},{6,30},{7,31},{8,16},{9,... | collective-permute-start | bytes 196616 | tf_op jit(solution)/shard_map/ppermute | solution.py:418
  57.4 0.4 collective-permute-done.19.refs_4_
  57.8 1.0 %gated_traces.2.refs_5_ = f32[8,160,256]{2,1,0:T(8,128)} custom-call(s32[160,256]{1,0:T(8,128)S(1)} %copy-done, bf16[96,512]{1,0:T(8,128)(2,1)S(1)} %get-tuple-element.63.refs_1_, bf16[96,512]{1,0:T(8,128)(2,1)S(1)} %collective-permute-done.17.refs_2_, bf16[96,512]{1,0:T(8,128)(2,1)S(1)} %collective-permute-done.18.refs_3_, ...), custom_call_target="tpu_custom_call" | custom-call | flops 500000000 | bytes 10000000 | tf_op jit(solution)/shard_map/gated_traces/pallas_call | solution.py:388
  58.9 0.2 collective-permute-done.14.refs_2_
  59.1 0.8 %collective-permute-done.16.refs_4_ = bf16[64,512]{1,0:T(8,128)(2,1)S(1)} collective-permute-done((bf16[64,512]{1,0:T(8,128)(2,1)S(1)}, bf16[64,512]{1,0:T(8,128)(2,1)S(1)}, u32[]{:S(2)}, u32[]{:S(2)}) %collective-permute-start.16) | collective-permute-done | bytes 65568 | tf_op jit(solution)/shard_map/ppermute | solution.py:418
  59.9 0.9 %gated_traces.3 = f32[8,160,256]{2,1,0:T(8,128)} custom-call(s32[160,256]{1,0:T(8,128)S(1)} %copy-done, bf16[64,512]{1,0:T(8,128)(2,1)S(1)} %get-tuple-element.59.refs_1_, bf16[64,512]{1,0:T(8,128)(2,1)S(1)} %collective-permute-done.14.refs_2_, bf16[64,512]{1,0:T(8,128)(2,1)S(1)} %collective-permute-done.15.refs_3_, ...), custom_call_target="tpu_custom_call", output_to_operand_aliasing={{}: (5, {})} | custom-call | flops 500000000 | bytes 10000000 | tf_op jit(solution)/shard_map/gated_traces/pallas_call | solution.py:388
  (25 shorter events, 0.3 us)
Async XLA Ops:
  2.4 12.1 %copy-start.2 = (s32[1,8,8]{2,1,0:T(8,128)S(1)}, s32[1,8,8]{2,1,0:T(8,128)}, u32[]{:S(2)}) copy-start(s32[1,8,8]{2,1,0:T(8,128)} %param.10) | copy-start | bytes 772
  3.6 7.3 %collective-permute-start.2 = (bf16[96,512]{1,0:T(8,128)(2,1)S(1)}, bf16[96,512]{1,0:T(8,128)(2,1)S(1)}, u32[]{:S(2)}, u32[]{:S(2)}) collective-permute-start(bf16[96,512]{1,0:T(8,128)(2,1)S(1)} %get-tuple-element.45), channel_id=1, source_target_pairs={{0,2},{1,3},{2,0},{3,1},{4,6},{5,7},{6,4},{7,5},{8,10},{9,11},{10,... | collective-permute-start | bytes 294920 | tf_op jit(solution)/shard_map/ppermute | solution.py:407
  6.8 4.9 %collective-permute-start.3 = (bf16[96,512]{1,0:T(8,128)(2,1)S(1)}, bf16[96,512]{1,0:T(8,128)(2,1)S(1)}, u32[]{:S(2)}, u32[]{:S(2)}) collective-permute-start(bf16[96,512]{1,0:T(8,128)(2,1)S(1)} %get-tuple-element.46), channel_id=1, source_target_pairs={{0,3},{1,2},{2,1},{3,0},{4,7},{5,6},{6,5},{7,4},{8,11},{9,10},{10,... | collective-permute-start | bytes 294920 | tf_op jit(solution)/shard_map/ppermute | solution.py:407
  6.8 11.8 %collective-permute-start.4 = (bf16[96,512]{1,0:T(8,128)(2,1)S(1)}, bf16[96,512]{1,0:T(8,128)(2,1)S(1)}, u32[]{:S(2)}, u32[]{:S(2)}) collective-permute-start(bf16[96,512]{1,0:T(8,128)(2,1)S(1)} %get-tuple-element.48), channel_id=1, source_target_pairs={{0,1},{1,0},{2,3},{3,2},{4,5},{5,4},{6,7},{7,6},{8,9},{9,8},{10,11... | collective-permute-start | bytes 294920 | tf_op jit(solution)/shard_map/ppermute | solution.py:407
  7.0 11.6 %collective-permute-start = (bf16[96,512]{1,0:T(8,128)(2,1)S(1)}, bf16[96,512]{1,0:T(8,128)(2,1)S(1)}, u32[]{:S(2)}, u32[]{:S(2)}) collective-permute-start(bf16[96,512]{1,0:T(8,128)(2,1)S(1)} %get-tuple-element.43), channel_id=1, source_target_pairs={{0,6},{1,7},{2,4},{3,5},{4,2},{5,3},{6,0},{7,1},{8,14},{9,15},{10,... | collective-permute-start | bytes 294920 | tf_op jit(solution)/shard_map/ppermute | solution.py:407
  10.9 7.6 %collective-permute-start.1 = (bf16[96,512]{1,0:T(8,128)(2,1)S(1)}, bf16[96,512]{1,0:T(8,128)(2,1)S(1)}, u32[]{:S(2)}, u32[]{:S(2)}) collective-permute-start(bf16[96,512]{1,0:T(8,128)(2,1)S(1)} %get-tuple-element.44), channel_id=1, source_target_pairs={{0,7},{1,6},{2,5},{3,4},{4,3},{5,2},{6,1},{7,0},{8,15},{9,14},{10,... | collective-permute-start | bytes 294920 | tf_op jit(solution)/shard_map/ppermute | solution.py:407
  10.9 14.6 %collective-permute-start.6 = (bf16[96,512]{1,0:T(8,128)(2,1)S(1)}, bf16[96,512]{1,0:T(8,128)(2,1)S(1)}, u32[]{:S(2)}, u32[]{:S(2)}) collective-permute-start(bf16[96,512]{1,0:T(8,128)(2,1)S(1)} %get-tuple-element.49), channel_id=1, source_target_pairs={{0,5},{1,4},{2,7},{3,6},{4,1},{5,0},{6,3},{7,2},{8,13},{9,12},{10,... | collective-permute-start | bytes 294920 | tf_op jit(solution)/shard_map/ppermute | solution.py:407
  11.7 16.1 %collective-permute-start.5 = (bf16[96,512]{1,0:T(8,128)(2,1)S(1)}, bf16[96,512]{1,0:T(8,128)(2,1)S(1)}, u32[]{:S(2)}, u32[]{:S(2)}) collective-permute-start(bf16[96,512]{1,0:T(8,128)(2,1)S(1)} %get-tuple-element.39.refs_2_), channel_id=1, source_target_pairs={{0,4},{1,5},{2,6},{3,7},{4,0},{5,1},{6,2},{7,3},{8,12},{9,13},{10,... | collective-permute-start | bytes 294920 | tf_op jit(solution)/shard_map/ppermute | solution.py:407
  18.5 9.2 %copy-start.1 = (bf16[1,2,640,256]{3,2,1,0:T(8,128)(2,1)S(1)}, bf16[1,2,640,256]{3,2,1,0:T(8,128)(2,1)}, u32[]{:S(2)}) copy-start(bf16[1,2,640,256]{3,2,1,0:T(8,128)(2,1)} %param.7) | copy-start | bytes 1966084
  29.6 9.6 %collective-permute-start.7 = (bf16[96,512]{1,0:T(8,128)(2,1)S(1)}, bf16[96,512]{1,0:T(8,128)(2,1)S(1)}, u32[]{:S(2)}, u32[]{:S(2)}) collective-permute-start(bf16[96,512]{1,0:T(8,128)(2,1)S(1)} %get-tuple-element.51), channel_id=1, source_target_pairs={{0,4},{1,5},{2,6},{3,7},{4,0},{5,1},{6,2},{7,3},{8,12},{9,13},{10,... | collective-permute-start | bytes 294920 | tf_op jit(solution)/shard_map/ppermute | solution.py:407
  29.7 11.2 %collective-permute-start.8 = (bf16[96,512]{1,0:T(8,128)(2,1)S(1)}, bf16[96,512]{1,0:T(8,128)(2,1)S(1)}, u32[]{:S(2)}, u32[]{:S(2)}) collective-permute-start(bf16[96,512]{1,0:T(8,128)(2,1)S(1)} %get-tuple-element.52), channel_id=1, source_target_pairs={{0,5},{1,4},{2,7},{3,6},{4,1},{5,0},{6,3},{7,2},{8,13},{9,12},{10,... | collective-permute-start | bytes 294920 | tf_op jit(solution)/shard_map/ppermute | solution.py:407
  31.9 14.4 %collective-permute-start.9 = (bf16[96,512]{1,0:T(8,128)(2,1)S(1)}, bf16[96,512]{1,0:T(8,128)(2,1)S(1)}, u32[]{:S(2)}, u32[]{:S(2)}) collective-permute-start(bf16[96,512]{1,0:T(8,128)(2,1)S(1)} %get-tuple-element.53), channel_id=1, source_target_pairs={{0,2},{1,3},{2,0},{3,1},{4,6},{5,7},{6,4},{7,5},{8,10},{9,11},{10,... | collective-permute-start | bytes 294920 | tf_op jit(solution)/shard_map/ppermute | solution.py:407
  32.7 13.6 %collective-permute-start.10 = (bf16[96,512]{1,0:T(8,128)(2,1)S(1)}, bf16[96,512]{1,0:T(8,128)(2,1)S(1)}, u32[]{:S(2)}, u32[]{:S(2)}) collective-permute-start(bf16[96,512]{1,0:T(8,128)(2,1)S(1)} %get-tuple-element.54), channel_id=1, source_target_pairs={{0,3},{1,2},{2,1},{3,0},{4,7},{5,6},{6,5},{7,4},{8,11},{9,10},{10,... | collective-permute-start | bytes 294920 | tf_op jit(solution)/shard_map/ppermute | solution.py:407
  34.0 12.3 %collective-permute-start.11 = (bf16[96,512]{1,0:T(8,128)(2,1)S(1)}, bf16[96,512]{1,0:T(8,128)(2,1)S(1)}, u32[]{:S(2)}, u32[]{:S(2)}) collective-permute-start(bf16[96,512]{1,0:T(8,128)(2,1)S(1)} %get-tuple-element.56), channel_id=1, source_target_pairs={{0,1},{1,0},{2,3},{3,2},{4,5},{5,4},{6,7},{7,6},{8,9},{9,8},{10,11... | collective-permute-start | bytes 294920 | tf_op jit(solution)/shard_map/ppermute | solution.py:407
  39.1 8.4 %collective-permute-start.12 = (bf16[96,512]{1,0:T(8,128)(2,1)S(1)}, bf16[96,512]{1,0:T(8,128)(2,1)S(1)}, u32[]{:S(2)}, u32[]{:S(2)}) collective-permute-start(bf16[96,512]{1,0:T(8,128)(2,1)S(1)} %get-tuple-element.57), channel_id=1, source_target_pairs={{0,6},{1,7},{2,4},{3,5},{4,2},{5,3},{6,0},{7,1},{8,14},{9,15},{10,... | collective-permute-start | bytes 294920 | tf_op jit(solution)/shard_map/ppermute | solution.py:407
  40.9 6.6 %collective-permute-start.13 = (bf16[96,512]{1,0:T(8,128)(2,1)S(1)}, bf16[96,512]{1,0:T(8,128)(2,1)S(1)}, u32[]{:S(2)}, u32[]{:S(2)}) collective-permute-start(bf16[96,512]{1,0:T(8,128)(2,1)S(1)} %get-tuple-element.58), channel_id=1, source_target_pairs={{0,7},{1,6},{2,5},{3,4},{4,3},{5,2},{6,1},{7,0},{8,15},{9,14},{10,... | collective-permute-start | bytes 294920 | tf_op jit(solution)/shard_map/ppermute | solution.py:407
  47.5 10.3 %copy-start = (s32[160,256]{1,0:T(8,128)S(1)}, s32[160,256]{1,0:T(8,128)}, u32[]{:S(2)}) copy-start(s32[160,256]{1,0:T(8,128)} %refs_0_.3) | copy-start | bytes 491524
  48.2 6.6 %collective-permute-start.17 = (bf16[96,512]{1,0:T(8,128)(2,1)S(1)}, bf16[96,512]{1,0:T(8,128)(2,1)S(1)}, u32[]{:S(2)}, u32[]{:S(2)}) collective-permute-start(bf16[96,512]{1,0:T(8,128)(2,1)S(1)} %get-tuple-element.64), channel_id=1, source_target_pairs={{0,16},{1,9},{2,18},{3,11},{4,20},{5,13},{6,22},{7,15},{8,24},{9,1... | collective-permute-start | bytes 294920 | tf_op jit(solution)/shard_map/ppermute | solution.py:418
  49.8 7.6 %collective-permute-start.18 = (bf16[96,512]{1,0:T(8,128)(2,1)S(1)}, bf16[96,512]{1,0:T(8,128)(2,1)S(1)}, u32[]{:S(2)}, u32[]{:S(2)}) collective-permute-start(bf16[96,512]{1,0:T(8,128)(2,1)S(1)} %get-tuple-element.65), channel_id=1, source_target_pairs={{0,8},{1,17},{2,10},{3,19},{4,12},{5,21},{6,14},{7,23},{8,0},{9,25... | collective-permute-start | bytes 294920 | tf_op jit(solution)/shard_map/ppermute | solution.py:418
  51.2 6.6 %collective-permute-start.19 = (bf16[96,512]{1,0:T(8,128)(2,1)S(1)}, bf16[96,512]{1,0:T(8,128)(2,1)S(1)}, u32[]{:S(2)}, u32[]{:S(2)}) collective-permute-start(bf16[96,512]{1,0:T(8,128)(2,1)S(1)} %get-tuple-element.66), channel_id=1, source_target_pairs={{0,24},{1,25},{2,26},{3,27},{4,28},{5,29},{6,30},{7,31},{8,16},{9,... | collective-permute-start | bytes 294920 | tf_op jit(solution)/shard_map/ppermute | solution.py:418
  51.7 7.4 %collective-permute-start.14 = (bf16[64,512]{1,0:T(8,128)(2,1)S(1)}, bf16[64,512]{1,0:T(8,128)(2,1)S(1)}, u32[]{:S(2)}, u32[]{:S(2)}) collective-permute-start(bf16[64,512]{1,0:T(8,128)(2,1)S(1)} %get-tuple-element.60), channel_id=1, source_target_pairs={{0,16},{1,9},{2,18},{3,11},{4,20},{5,13},{6,22},{7,15},{8,24},{9,1... | collective-permute-start | bytes 196616 | tf_op jit(solution)/shard_map/ppermute | solution.py:418
  53.2 5.8 %collective-permute-start.15 = (bf16[64,512]{1,0:T(8,128)(2,1)S(1)}, bf16[64,512]{1,0:T(8,128)(2,1)S(1)}, u32[]{:S(2)}, u32[]{:S(2)}) collective-permute-start(bf16[64,512]{1,0:T(8,128)(2,1)S(1)} %get-tuple-element.61), channel_id=1, source_target_pairs={{0,8},{1,17},{2,10},{3,19},{4,12},{5,21},{6,14},{7,23},{8,0},{9,25... | collective-permute-start | bytes 196616 | tf_op jit(solution)/shard_map/ppermute | solution.py:418
  54.7 5.2 %collective-permute-start.16 = (bf16[64,512]{1,0:T(8,128)(2,1)S(1)}, bf16[64,512]{1,0:T(8,128)(2,1)S(1)}, u32[]{:S(2)}, u32[]{:S(2)}) collective-permute-start(bf16[64,512]{1,0:T(8,128)(2,1)S(1)} %get-tuple-element.62), channel_id=1, source_target_pairs={{0,24},{1,25},{2,26},{3,27},{4,28},{5,29},{6,30},{7,31},{8,16},{9,... | collective-permute-start | bytes 196616 | tf_op jit(solution)/shard_map/ppermute | solution.py:418
